TPU v7x, 512 devices: a whole 4x8x8 slice. The times are simulated.
512 devices in a mesh: seq: 32 (over y, x), chan: 16 (over z, core).
Axes of the slice: x: 4, y: 8, z: 8, core: 2. Of those that a mesh axis runs over, the one named last changes fastest.
Arguments:
- tokens: bfloat16 [8192, 2048], P(('seq', 'chan')), may hold values from -6 to 6
- norm_gain: float32 [2048], replicated, may hold values from 0.1 to 1.9
- entry_projection_matrix: bfloat16 [2, 2048, 4096], P(None, None, 'chan'), may hold values from -0.125 to 0.125
- conv_weight: float32 [4, 4096], P(None, 'chan'), may hold values from -3 to 3
- conv_bias: float32 [4096], P('chan'), may hold values from -3 to 3
- w_x: bfloat16 [4096, 160], P('chan'), may hold values from -0.09375 to 0.09375
- timescale_matrix: bfloat16 [128, 4096], P(None, 'chan'), may hold values from -0.5 to 0.5
- timescale_offset: float32 [4096], P('chan'), may hold values from -8 to -2
- a_log: float32 [16, 4096], P(None, 'chan'), may hold values from -1 to 2.77
- skip_gain: float32 [4096], P('chan'), may hold values from 0.5 to 1.5
- w_out: bfloat16 [4096, 2048], P('chan'), may hold values from -0.09375 to 0.09375
- lengths: int32 [4], replicated, may hold values from 1 to 4096, 7936 in all
- req_order: int32 [4], replicated, may hold values from 0 to 3, each once
Outputs:
- mixed: bfloat16 [8192, 2048], P(('seq', 'chan'))
- last_states: float32 [4, 16, 4096], P(None, None, ('chan', 'seq'))
- conv_edges: bfloat16 [4, 4, 4096], P(None, None, ('chan', 'seq'))
Inputs may be any that keep to these rules, and one draw needn't show every extreme that they name: The lengths sum to exactly 7936, and the longest is exactly 4096. `req_order`: each request appears exactly once.
All inputs are finite; a program needn't handle non-finite values.
Results may differ from a plain program's by a relative error of at most 0.0095.
Values may be sent and summed in bfloat16 or wider, within the bound.
No kernel may reach another device: no remote copies, remote signals or barrier semaphores. Data moves between devices by JAX's collectives and lax.ppermute only.
A program may use at most 64 MiB of HBM per device.

v0:
```python
import jax
import jax.numpy as jnp
from jax import lax
from jax.sharding import PartitionSpec as P

STRETCH = 64


def shifted(block, axis, distance):
    devices = range(lax.axis_size(axis))
    route = [(i - distance, i) for i in devices if i - distance in devices]
    return lax.ppermute(block, axis, route)


def sequence_arrangement(lengths, req_order, slot_ids):
    req_count = lengths.shape[0]
    req_index = jnp.arange(req_count, dtype=jnp.int32)
    filled_length_total = (lengths + STRETCH - 1) // STRETCH * STRETCH
    pick_order = (req_order[:, None] == req_index[None, :]).astype(jnp.int32)
    placed_pad = jnp.sum(pick_order * filled_length_total[None, :], axis=1)
    placed_len = jnp.sum(pick_order * lengths[None, :], axis=1)
    end_slots = jnp.cumsum(placed_pad)
    begin_slots = end_slots - placed_pad
    sequence_beginnings = jnp.sum(pick_order * begin_slots[:, None], axis=0)
    inside = (slot_ids[:, None] >= begin_slots[None, :]) & (slot_ids[:, None] < end_slots[None, :])
    slot_owner = jnp.sum(jnp.where(inside, req_index[None, :] + 1, 0), axis=1)
    slot_owner = jnp.where(slot_ids < 0, -1, slot_owner)
    in_request = inside & (slot_ids[:, None] - begin_slots[None, :] < placed_len[None, :])
    present_flag = jnp.sum(jnp.where(in_request, 1, 0), axis=1).astype(jnp.int32)
    return (filled_length_total, sequence_beginnings, slot_owner, present_flag)


def chain_pair(earlier, later):
    return (earlier[0] * later[0], later[0] * earlier[1] + later[1])


def on_device(
    tokens,
    norm_gain,
    entry_projection_matrix,
    conv_weight,
    conv_bias,
    w_x,
    timescale_matrix,
    timescale_offset,
    a_log,
    skip_gain,
    w_out,
    lengths,
    req_order,
):
    tok_rows = tokens.shape[0]
    seq_rows = tok_rows * lax.axis_size("chan")
    chan_width = entry_projection_matrix.shape[2]
    state_size = a_log.shape[0]
    rank_size = timescale_matrix.shape[0]
    halo_count = conv_weight.shape[0] - 1
    req_count = lengths.shape[0]
    base_slot = lax.axis_index("seq") * seq_rows
    ext_slots = base_slot - halo_count + jnp.arange(seq_rows + halo_count, dtype=jnp.int32)
    filled_length_total, sequence_beginnings, padded_request_owner, widened_presence_mask = (
        sequence_arrangement(lengths, req_order, ext_slots)
    )
    slot_owner = padded_request_owner[halo_count:]
    position_presence = widened_presence_mask[halo_count:].astype(jnp.float32)
    widened = tokens.astype(jnp.float32)
    scale_row = lax.rsqrt(jnp.mean(widened * widened, axis=1, keepdims=True) + 1e-05)
    rescaled_entries = (widened * scale_row * norm_gain[None, :]).astype(jnp.bfloat16)
    mapped_signal = jnp.einsum(
        "td,kde->kte",
        lax.all_gather(rescaled_entries, "chan", axis=0, tiled=True),
        entry_projection_matrix,
        preferred_element_type=jnp.float32,
    )
    mixer_signal = (mapped_signal[0] * position_presence[:, None]).astype(jnp.bfloat16)
    switch_signal = mapped_signal[1].astype(jnp.bfloat16)
    rim_rows = shifted(mixer_signal[seq_rows - halo_count :], "seq", 1)
    extended = jnp.concatenate([rim_rows, mixer_signal], axis=0).astype(jnp.float32)
    conv_sum = conv_bias[None, :] + jnp.zeros((seq_rows, chan_width), jnp.float32)
    for shift_by in range(halo_count + 1):
        lower = halo_count - shift_by
        same_req = (padded_request_owner[lower : lower + seq_rows] == slot_owner).astype(
            jnp.float32
        )
        conv_sum = (
            conv_sum
            + conv_weight[lower][None, :] * extended[lower : lower + seq_rows] * same_req[:, None]
        )
    activated = jax.nn.silu(conv_sum).astype(jnp.bfloat16)
    x_proj = lax.psum(jnp.dot(activated, w_x, preferred_element_type=jnp.float32), "chan")
    thin_timescale_factor = x_proj[:, :rank_size].astype(jnp.bfloat16)
    in_coef = x_proj[:, rank_size : rank_size + state_size]
    out_coef = x_proj[:, rank_size + state_size :]
    timescale_values = position_presence[:, None] * jax.nn.softplus(
        jnp.dot(thin_timescale_factor, timescale_matrix, preferred_element_type=jnp.float32)
        + timescale_offset[None, :]
    )
    decay_rate = -jnp.exp(a_log)
    keep_flag = (
        padded_request_owner[halo_count - 1 : halo_count - 1 + seq_rows] == slot_owner
    ).astype(jnp.float32)
    act_wide = activated.astype(jnp.float32)
    block_len = min(16, STRETCH)
    block_count = seq_rows // block_len

    def arrange(values):
        return jnp.swapaxes(values.reshape((block_count, block_len) + values.shape[1:]), 0, 1)

    def advance(running, slot_in):
        state_now, decay_now = running
        step_delta, step_input, step_in, step_out, step_keep = slot_in
        factor = step_keep[:, None, None] * jnp.exp(step_delta[:, None, :] * decay_rate[None])
        state_now = factor * state_now + (step_delta * step_input)[:, None, :] * step_in[:, :, None]
        decay_now = factor * decay_now
        local_out = jnp.sum(step_out[:, :, None] * state_now, axis=1)
        return ((state_now, decay_now), (local_out, step_out[:, :, None] * decay_now))

    empty_state = jnp.zeros((block_count, state_size, chan_width), jnp.float32)
    slot_in = (
        arrange(timescale_values),
        arrange(act_wide),
        arrange(in_coef),
        arrange(out_coef),
        arrange(keep_flag),
    )
    (block_state, block_decay), (local_y, weighted) = lax.scan(
        advance, (empty_state, jnp.ones_like(empty_state)), slot_in
    )
    incl_decay, incl_state = lax.associative_scan(chain_pair, (block_decay, block_state), axis=0)
    own_decay = incl_decay[-1]
    own_state = incl_state[-1]

    def relay(relay_turn, incoming):
        return shifted(own_decay * incoming + own_state, "seq", 1)

    incoming = lax.fori_loop(0, lax.axis_size("seq") - 1, relay, jnp.zeros_like(own_state))
    start_decay = jnp.concatenate([jnp.ones_like(incl_decay[:1]), incl_decay[:-1]], axis=0)
    start_state = jnp.concatenate([jnp.zeros_like(incl_state[:1]), incl_state[:-1]], axis=0)
    begin_state = start_decay * incoming[None] + start_state
    end_state = incl_decay * incoming[None] + incl_state
    carried = jnp.sum(weighted * begin_state[None], axis=2)
    complete_result = (
        jnp.swapaxes(local_y + carried, 0, 1).reshape(seq_rows, chan_width)
        + skip_gain[None, :] * act_wide
    )
    switched_result = (
        position_presence[:, None]
        * complete_result
        * jax.nn.silu(switch_signal.astype(jnp.float32))
    ).astype(jnp.bfloat16)
    summed = lax.psum_scatter(
        jnp.dot(switched_result, w_out, preferred_element_type=jnp.float32),
        "chan",
        scatter_dimension=0,
        tiled=True,
    )
    mixed = (widened + summed).astype(jnp.bfloat16)
    block_ends = base_slot + (jnp.arange(block_count, dtype=jnp.int32) + 1) * block_len - 1
    final_hits = (
        (sequence_beginnings + filled_length_total - 1)[:, None] == block_ends[None, :]
    ).astype(jnp.float32)
    state_part = jnp.einsum("rb,bne->rne", final_hits, end_state, precision=lax.Precision.HIGHEST)
    slots_here = base_slot + jnp.arange(seq_rows, dtype=jnp.int32)
    offsets = jnp.arange(halo_count + 1, dtype=jnp.int32)
    back_pos = lengths[:, None] - (halo_count + 1) + offsets[None, :]
    target = sequence_beginnings[:, None] + back_pos
    picked = (target[:, :, None] == slots_here[None, None, :]) & (back_pos >= 0)[:, :, None]
    pick_matrix = picked.astype(jnp.bfloat16).reshape(req_count * (halo_count + 1), seq_rows)
    edge_part = jnp.dot(pick_matrix, mixer_signal, preferred_element_type=jnp.float32).reshape(
        req_count, halo_count + 1, chan_width
    )
    last_states, edge_sums = (
        lax.psum_scatter(state_part, "seq", scatter_dimension=2, tiled=True),
        lax.psum_scatter(edge_part, "seq", scatter_dimension=2, tiled=True),
    )
    return (mixed, last_states, edge_sums.astype(jnp.bfloat16))


def solution(mesh):
    in_specs = (
        P(("seq", "chan"), None),
        P(),
        P(None, None, "chan"),
        P(None, "chan"),
        P("chan"),
        P("chan", None),
        P(None, "chan"),
        P("chan"),
        P(None, "chan"),
        P("chan"),
        P("chan", None),
        P(),
        P(),
    )
    out_specs = (
        P(("seq", "chan"), None),
        P(None, None, ("chan", "seq")),
        P(None, None, ("chan", "seq")),
    )
    return jax.shard_map(
        on_device, mesh=mesh, in_specs=in_specs, out_specs=out_specs, check_vma=False
    )
```

profile of v0, /device:TPU:1, one launch (start us, length us, event | category | flops | bytes accessed | tf_op | source)
XLA Modules:
  0.0 753.7 jit_solution(17366890487351695271)
XLA Ops:
  7.3 1.1 fusion.20
  8.4 1.6 fusion.22
  10.0 1.2 broadcast_add_fusion
  12.2 0.9 select_reduce_fusion.2
  14.9 43.6 %all-gather.2.cloned.1.call-done = bf16[256,2048]{1,0:T(8,128)(2,1)} async-done(((bf16[16,2048]{1,0:T(8,128)(2,1)}), bf16[256,2048]{1,0:T(8,128)(2,1)}) %all-gather.2.cloned.1.call-update) | async-done | bytes 1048592 | tf_op jit(solution)/shard_map/all_gather | solution.py:71
  58.5 1.9 convolution_bitcast_fusion
  61.4 3.1 collective-permute-start.1
  65.5 0.9 fusion.53
  67.7 108.7 %all-reduce.23.cloned.1.call-done = f32[256,160]{0,1:T(8,128)} async-done(((f32[256,160]{0,1:T(8,128)}), f32[256,160]{0,1:T(8,128)}) %all-reduce.23.cloned.1.call-update) | async-done | bytes 163856 | tf_op jit(solution)/shard_map/psum | solution.py:90
  176.4 1.2 fusion.7
  179.7 49.3 %while.28 = (s32[]{:T(128)}, f32[16,16,256]{2,1,0:T(8,128)S(1)}, f32[16,16,256]{2,1,0:T(8,128)S(1)}, f32[16,16,256]{2,1,0:T(8,128)}, f32[16,16,16,256]{3,2,1,0:T...) while((s32[]{:T(128)}, f32[16,16,256]{2,1,0:T(8,128)S(1)}, ...), condition=%wide.region_9.10_spmd.clone, body=%wide.region_7.9_spmd.clone.sunk | while | flops 851971 | bytes 1532312 | solution.py:126
  192.7 0.8 bitcast_dynamic-update-slice_fusion.4
  202.0 0.9 bitcast_dynamic-update-slice_fusion.4
  214.3 0.9 bitcast_dynamic-update-slice_fusion.4
  223.6 0.8 bitcast_dynamic-update-slice_fusion.4
  235.8 2.9 pad.59
  238.7 1.6 pad_maximum_fusion
  240.3 2.9 pad.58
  244.0 194.5 %while.27 = (s32[]{:T(128)}, f32[16,256]{1,0:T(8,128)S(1)}, f32[16,256]{1,0:T(8,128)S(1)}, f32[16,256]{1,0:T(8,128)S(1)}, s32[]{:T(128)}) while((s32[]{:T(128)}, f32[16,256]{1,0:T(8,128)S(1)}, f32[16,256]{1,0:T(8,128)S(1)}, f32[16,256]{1,0:T(8,128)S(1)}, s32[]{:T(128)}) %tuple.80), condition=%wide.region_11.12_spmd, body=%wide.region_10.11_spmd.sunk | while | flops 8194 | bytes 131173 | solution.py:136
  244.0 3.1 collective-permute-start
  247.1 0.8 collective-permute-done
  247.9 3.6 collective-permute-start
  251.5 0.8 collective-permute-done
  252.4 3.6 collective-permute-start
  256.9 3.6 collective-permute-start
  261.3 3.8 collective-permute-start
  266.0 5.7 collective-permute-start
  272.6 5.7 collective-permute-start
  279.2 5.7 collective-permute-start
  285.8 5.7 collective-permute-start
  292.4 5.7 collective-permute-start
  299.0 6.0 collective-permute-start
  305.9 5.7 collective-permute-start
  312.5 5.7 collective-permute-start
  319.0 5.7 collective-permute-start
  325.6 5.7 collective-permute-start
  332.2 5.7 collective-permute-start
  338.8 5.7 collective-permute-start
  345.4 6.2 collective-permute-start
  352.4 5.7 collective-permute-start
  359.0 5.7 collective-permute-start
  365.6 5.7 collective-permute-start
  372.2 5.7 collective-permute-start
  378.8 5.7 collective-permute-start
  385.4 5.7 collective-permute-start
  392.0 6.2 collective-permute-start
  399.0 5.7 collective-permute-start
  405.6 5.7 collective-permute-start
  412.2 5.7 collective-permute-start
  418.7 5.7 collective-permute-start
  425.3 5.7 collective-permute-start
  431.9 5.7 collective-permute-start
  438.5 1.3 multiply_add_fusion.1
  439.8 3.4 multiply_reduce_fusion.1
  443.2 0.9 copy.45
  444.5 1.0 copy.47
  445.6 1.4 fusion.19
  447.0 1.8 fusion.54
  448.8 1.3 dynamic-slice
  452.1 1.2 fusion.25
  453.3 142.2 %all-reduce.19 = bf16[4,4,256]{2,1,0:T(4,128)(2,1)S(1)} all-reduce(f32[4,4,256]{2,1,0:T(4,128)S(1)} %fusion.25), channel_id=4, replica_groups=mesh['seq'=32,'chan'=16] {'seq'}, use_global_device_ids=true, to_apply=%region_16.17.clone | all-reduce | flops 4096 | bytes 24576
  596.1 84.2 %all-reduce.25.cloned.1.call-done = f32[4,16,256]{1,0,2:T(4,128)} async-done(((f32[4,16,256]{1,0,2:T(4,128)}), f32[4,16,256]{1,0,2:T(4,128)}) %all-reduce.25.cloned.1.call-update) | async-done | bytes 65552
  681.6 64.0 %reduce-scatter.3.cloned.1.call-done = f32[16,2048]{1,0:T(8,128)} async-done(((f32[256,2048]{1,0:T(8,128)}), f32[16,2048]{1,0:T(8,128)}) %reduce-scatter.3.cloned.1.call-update) | async-done | bytes 131088 | tf_op jit(solution)/shard_map/reduce_scatter | solution.py:151
  745.6 1.6 fusion.23
  (288 shorter events, 89.9 us)
Async XLA Ops:
  7.2 51.4 %copy-start = (bf16[2,2048,256]{2,1,0:T(8,128)(2,1)S(1)}, bf16[2,2048,256]{2,1,0:T(8,128)(2,1)}, u32[]{:S(2)}) copy-start(bf16[2,2048,256]{2,1,0:T(8,128)(2,1)} %param.19) | copy-start | bytes 6291460
  7.2 58.0 %copy-start.12 = (f32[256]{0:T(256)S(1)}, f32[256]{0:T(256)}, u32[]{:S(2)}) copy-start(f32[256]{0:T(256)} %param.21) | copy-start | bytes 3076
  7.2 58.3 %copy-start.5 = (bf16[256,160]{0,1:T(8,128)(2,1)S(1)}, bf16[256,160]{0,1:T(8,128)(2,1)}, u32[]{:S(2)}) copy-start(bf16[256,160]{0,1:T(8,128)(2,1)} %param.22) | copy-start | bytes 245764
  7.2 169.2 %copy-start.16 = (bf16[128,256]{1,0:T(8,128)(2,1)S(1)}, bf16[128,256]{1,0:T(8,128)(2,1)}, u32[]{:S(2)}) copy-start(bf16[128,256]{1,0:T(8,128)(2,1)} %param.23) | copy-start | bytes 196612
  7.2 169.2 %copy-start.17 = (f32[256]{0:T(256)S(1)}, f32[256]{0:T(256)}, u32[]{:S(2)}) copy-start(f32[256]{0:T(256)} %param.24) | copy-start | bytes 3076
  7.2 51.3 %all-gather.2.cloned.1.call-start = ((), (), s32[]{:S(2)}) async-start(), calls=%async_computation.1 | async-start | bytes 1114112 | tf_op jit(solution)/shard_map/all_gather | solution.py:71
  10.0 166.4 %all-reduce.23.cloned.1.call-start = ((), (), s32[]{:S(2)}) async-start(), calls=%async_computation.2 | async-start | bytes 327680 | tf_op jit(solution)/shard_map/psum | solution.py:90
  13.1 165.6 %copy-start.13 = (s32[4]{0:T(128)}, s32[4]{0:T(128)S(1)}, u32[]{:S(2)}) copy-start(s32[4]{0:T(128)S(1)} %get-tuple-element.173) | copy-start | bytes 52
  13.3 164.3 %copy-start.6 = (f32[256]{0:T(256)}, f32[256]{0:T(256)S(1)}, u32[]{:S(2)}) copy-start(f32[256]{0:T(256)S(1)} %get-tuple-element.237) | copy-start | bytes 3076
  13.3 164.3 %copy-start.7 = (f32[256]{0:T(256)}, f32[256]{0:T(256)S(1)}, u32[]{:S(2)}) copy-start(f32[256]{0:T(256)S(1)} %get-tuple-element.238) | copy-start | bytes 3076
  14.2 163.5 %copy-start.8 = (f32[1,256]{1,0:T(1,128)}, f32[1,256]{1,0:T(1,128)S(1)}, u32[]{:S(2)}) copy-start(f32[1,256]{1,0:T(1,128)S(1)} %get-tuple-element.233) | copy-start | bytes 3076
  14.2 163.5 %copy-start.9 = (f32[1,256]{1,0:T(1,128)}, f32[1,256]{1,0:T(1,128)S(1)}, u32[]{:S(2)}) copy-start(f32[1,256]{1,0:T(1,128)S(1)} %get-tuple-element.234) | copy-start | bytes 3076
  14.2 163.5 %copy-start.10 = (f32[1,256]{1,0:T(1,128)}, f32[1,256]{1,0:T(1,128)S(1)}, u32[]{:S(2)}) copy-start(f32[1,256]{1,0:T(1,128)S(1)} %get-tuple-element.235) | copy-start | bytes 3076
  14.2 163.5 %copy-start.11 = (f32[1,256]{1,0:T(1,128)}, f32[1,256]{1,0:T(1,128)S(1)}, u32[]{:S(2)}) copy-start(f32[1,256]{1,0:T(1,128)S(1)} %get-tuple-element.236) | copy-start | bytes 3076
  60.5 0.8 copy-start.2
  61.4 3.8 collective-permute-start.1
  66.4 613.9 %all-reduce.25.cloned.1.call-start = ((), (), s32[]{:S(2)}) async-start(), calls=%async_computation.4 | async-start | bytes 1048576
  244.0 3.9 collective-permute-start
  247.9 4.5 collective-permute-start
  252.4 4.5 collective-permute-start
  256.9 4.5 collective-permute-start
  261.3 4.7 collective-permute-start
  266.0 6.6 collective-permute-start
  272.6 6.6 collective-permute-start
  279.2 6.6 collective-permute-start
  285.8 6.6 collective-permute-start
  292.4 6.6 collective-permute-start
  299.0 6.9 collective-permute-start
  305.9 6.6 collective-permute-start
  312.5 6.6 collective-permute-start
  319.0 6.6 collective-permute-start
  325.6 6.6 collective-permute-start
  332.2 6.6 collective-permute-start
  338.8 6.6 collective-permute-start
  345.4 7.0 collective-permute-start
  352.4 6.6 collective-permute-start
  359.0 6.6 collective-permute-start
  365.6 6.6 collective-permute-start
  372.2 6.6 collective-permute-start
  378.8 6.6 collective-permute-start
  385.4 6.6 collective-permute-start
  392.0 7.0 collective-permute-start
  399.0 6.6 collective-permute-start
  405.6 6.6 collective-permute-start
  412.2 6.6 collective-permute-start
  418.7 6.6 collective-permute-start
  425.3 6.6 collective-permute-start
  431.9 6.6 collective-permute-start
  438.5 4.7 copy-start.4
  438.5 5.6 copy-start.14
  438.5 5.6 copy-start.15
  439.8 7.2 copy-start.1
  444.5 301.2 %copy-start.3 = (bf16[16,2048]{1,0:T(8,128)(2,1)S(1)}, bf16[16,2048]{1,0:T(8,128)(2,1)}, u32[]{:S(2)}) copy-start(bf16[16,2048]{1,0:T(8,128)(2,1)} %param.17) | copy-start | bytes 196612
  445.5 300.1 %reduce-scatter.3.cloned.1.call-start = ((), (), s32[]{:S(2)}) async-start(), calls=%async_computation.3 | async-start | bytes 2228224 | tf_op jit(solution)/shard_map/reduce_scatter | solution.py:151
Sparse Core Ops, SparseCore 0:
  10.7 47.7 all-gather.1
  66.5 109.8 all-reduce.22
  445.6 234.5 all-reduce.24
  683.0 62.6 reduce-scatter.2
where the time goes:
time: 760 us; the launch traced here: 754 us
  waiting for transfers between devices  327 us (43%)
  starting transfers between devices  171 us (22%)
  blocking collectives  142 us (19%)
  other arithmetic  52.1 us (7%)
  local copies, waits for them, and re-layouts  38.7 us (5%)
  between operations  14.9 us (2%)
    ppermute x32, starting transfers between devices, shifted(): return lax.ppermute(block, axis, route)  171 us
    unnamed x1, blocking collectives  142 us
    psum x1, waiting for transfers between devices, on_device(): lax.psum(jnp.dot(activated, w_x, preferred_element_type=jnp.float32), 'ch...  109 us
    unnamed x5, waiting for transfers between devices  84.2 us
    reduce_scatter x1, waiting for transfers between devices, on_device(): lax.psum_scatter(jnp.dot(switched_result, w_out, preferred_element_type=j...  64 us
    all_gather x1, waiting for transfers between devices, on_device(): lax.all_gather(rescaled_entries, 'chan', axis=0, tiled=True)  43.6 us
    ppermute x32, waiting for transfers between devices, shifted(): return lax.ppermute(block, axis, route)  26.3 us
  transfers between devices with their start and end apart: 36, of which 35 were waited for; matrix products, arithmetic and copies ran while one was open for 2% of the time, Pallas kernels for 0%

commit v1 on v0

v1 whole, which is shorter than its diff:
```python
import functools

import jax
import jax.numpy as jnp
from jax import lax
from jax.experimental import pallas as pl
from jax.experimental.pallas import tpu as pltpu
from jax.sharding import PartitionSpec as P

STRETCH = 64
BLOCKS = 8
LOG2E = 1.4426950408889634
F32 = jnp.float32
BF16 = jnp.bfloat16
HALO = 8


def placements(lengths_ref, order_ref):
    out = []
    position = jnp.int32(0)
    for i in range(lengths_ref.shape[0]):
        request = order_ref[i]
        length = lengths_ref[request]
        begin = position
        position = begin + (length + STRETCH - 1) // STRETCH * STRETCH
        out.append((request, begin, length, position))
    return out


def live_rows(laid, slots):
    live = jnp.zeros(slots.shape, jnp.bool_)
    for _, begin, length, _ in laid:
        live = live | ((slots >= begin) & (slots < begin + length))
    return live


def opens(laid, slots):
    hit = slots == laid[-1][3]
    for _, begin, _, _ in laid:
        hit = hit | (slots == begin)
    return hit


def norm_kernel(copies, tokens_ref, gain_ref, out_ref):
    wide = tokens_ref[...].astype(F32)
    scale = lax.rsqrt(jnp.mean(wide * wide, axis=1, keepdims=True) + 1e-05)
    normed = (wide * scale * gain_ref[...]).astype(BF16)
    for i in range(copies):
        out_ref[i] = normed


def entry_kernel(rows, lengths_ref, order_ref, own_ref, other_ref, weight_ref, inner_ref, gate_ref, tail_ref):
    core = lax.rem(lax.axis_index("chan"), 2)
    span = inner_ref.shape[0]
    base = lax.axis_index("seq") * span
    laid = placements(lengths_ref, order_ref)
    live = live_rows(laid, base + lax.broadcasted_iota(jnp.int32, (span, 1), 0))
    other = other_ref[...]
    first = core == 0
    arranged = []
    for k in range(2):
        own_part = own_ref[k]
        other_part = jnp.dot(other, weight_ref[k], preferred_element_type=F32)
        low = jnp.where(first, own_part, other_part)
        high = jnp.where(first, other_part, own_part)
        pieces = []
        for z in range(span // (2 * rows)):
            pieces += [low[z * rows : (z + 1) * rows], high[z * rows : (z + 1) * rows]]
        arranged.append(jnp.concatenate(pieces, axis=0))
    inner = jnp.where(live, arranged[0], 0.0)
    inner_ref[...] = inner.astype(BF16)
    tail_ref[...] = inner[span - HALO :].astype(BF16)
    gate = arranged[1].astype(BF16).astype(F32)
    gate_ref[...] = jnp.where(live, gate / (1.0 + jnp.exp(-gate)), 0.0)


def conv_kernel(lengths_ref, order_ref, inner_ref, halo_ref, taps_ref, bias_ref, wx_ref, act_ref, part_ref, edge_ref):
    span, width = inner_ref.shape
    base = lax.axis_index("seq") * span
    laid = placements(lengths_ref, order_ref)
    taps = taps_ref.shape[0]
    inner = inner_ref[...]
    wide = inner.astype(F32)
    before = halo_ref[...].astype(F32)
    for q in range(span // STRETCH):
        here = wide[q * STRETCH : (q + 1) * STRETCH]
        fresh = opens(laid, base + q * STRETCH)
        before = jnp.where(fresh, 0.0, before)
        extended = jnp.concatenate([before, here], axis=0)
        total = jnp.broadcast_to(bias_ref[...], here.shape)
        for k in range(taps - 1, -1, -1):
            shift = HALO - (taps - 1 - k)
            total = total + taps_ref[k : k + 1, :] * extended[shift : shift + STRETCH]
        act_ref[pl.ds(q * STRETCH, STRETCH), :] = (total / (1.0 + jnp.exp(-total))).astype(BF16)
        before = here[STRETCH - HALO :]
    part_ref[...] = jnp.dot(act_ref[...], wx_ref[...], preferred_element_type=F32).astype(BF16)
    column = lax.broadcasted_iota(jnp.int32, (1, 128), 1)
    target = jnp.full((1, 128), -1, jnp.int32)
    for request, begin, length, _ in laid:
        back = length - taps + (column - request * taps)
        mine = (column >= request * taps) & (column < request * taps + taps) & (back >= 0)
        target = jnp.where(mine, begin + back, target)
    slots = base + lax.broadcasted_iota(jnp.int32, (span, 128), 0)
    pick = (slots == target).astype(F32).astype(BF16)
    edge_ref[...] = lax.dot_general(inner, pick, (((0,), (0,)), ((), ())), preferred_element_type=F32)


def share_kernel(copies, parts_ref, out_ref):
    total = jnp.sum(parts_ref[...].astype(F32), axis=0).astype(BF16)
    for i in range(copies):
        out_ref[i] = total


def put(ref, values):
    for h in range(ref.shape[0]):
        ref[h] = values[:, h * 128 : (h + 1) * 128]


def every(ref, t, steps):
    return jnp.concatenate([ref[h, pl.ds(t, BLOCKS, stride=steps), :] for h in range(ref.shape[0])], axis=1)


def spread(values, n):
    return jnp.broadcast_to(values[:, n : n + 1], (BLOCKS, 128))


def twice(values, width):
    return jnp.concatenate([values] * (width // 128), axis=1)


def local_kernel(lengths_ref, order_ref, xp_ref, tm_ref, off_ref, act_ref, alog_ref, send_ref, delta_ref, drive_ref, rate_ref, coef_ref):
    span, width = act_ref.shape
    states = alog_ref.shape[0]
    rank = tm_ref.shape[0]
    steps = span // BLOCKS
    base = lax.axis_index("seq") * span
    laid = placements(lengths_ref, order_ref)
    live = live_rows(laid, base + lax.broadcasted_iota(jnp.int32, (span, 1), 0))
    xp = xp_ref[...]
    raw = jnp.dot(xp[:, :rank], tm_ref[...], preferred_element_type=F32) + off_ref[...]
    soft = jnp.maximum(raw, 0.0) + jnp.log1p(jnp.exp(-jnp.abs(raw)))
    delta = jnp.where(live, soft, 0.0)
    put(delta_ref, delta)
    put(drive_ref, delta * act_ref[...].astype(F32))
    coef = xp[:, rank:].astype(F32)
    coef_ref[...] = jnp.concatenate([coef, jnp.zeros((span, 128 - coef.shape[1]), F32)], axis=1)
    rate = -jnp.exp(alog_ref[...]) * LOG2E
    for n in range(states):
        rate_ref[n] = jnp.broadcast_to(rate[n : n + 1], (BLOCKS, width))

    def step(t, carry):
        total, state = carry
        now = every(delta_ref, t, steps)
        push = every(drive_ref, t, steps)
        coefs = coef_ref[pl.ds(t, BLOCKS, stride=steps), :]
        moved = []
        for n in range(states):
            moved.append(jnp.exp2(now * rate_ref[n]) * state[n] + push * twice(spread(coefs, n), width))
        return (total + now, tuple(moved))

    zero = jnp.zeros((BLOCKS, width), F32)
    total, state = lax.fori_loop(0, steps, step, (zero, (zero,) * states), unroll=2)
    dests, both, _ = send_ref.shape
    sub = both // 2
    send_ref[:, :sub, :] = jnp.concatenate(state, axis=0).T.reshape(dests, sub, states * BLOCKS)
    decay = [jnp.exp2(total * rate_ref[n]) for n in range(states)]
    send_ref[:, sub:, :] = jnp.concatenate(decay, axis=0).T.reshape(dests, sub, states * BLOCKS)


def chain_kernel(steps, lengths_ref, order_ref, got_ref, edge_ref, back_ref, last_ref, run_ref, tot_ref, all_ref, hold_ref):
    spans, both, lanes = got_ref.shape
    sub = both // 2
    states = lanes // BLOCKS
    laid = placements(lengths_ref, order_ref)
    block = lax.broadcasted_iota(jnp.int32, (1, 1, lanes), 2) % BLOCKS
    index = lax.broadcasted_iota(jnp.int32, (spans, 1, lanes), 0) * BLOCKS + block
    keep = jnp.where(opens(laid, index * steps), 0.0, 1.0)
    state = got_ref[:, :sub, :]
    decay = got_ref[:, sub:, :] * keep
    shift = 1
    while shift < BLOCKS:
        within = block >= shift
        prev_state = jnp.where(within, pltpu.roll(state, shift, 2), 0.0)
        prev_decay = jnp.where(within, pltpu.roll(decay, shift, 2), 1.0)
        state = state + decay * prev_state
        decay = decay * prev_decay
        shift *= 2

    def replicate(values):
        values = jnp.where(block == BLOCKS - 1, values, 0.0)
        shift = 1
        while shift < BLOCKS:
            values = values + pltpu.roll(values, lanes - shift, 2)
            shift *= 2
        return values

    run_ref[...] = replicate(state)
    tot_ref[...] = replicate(decay)
    entering = jnp.zeros((sub, lanes), F32)
    for s in range(spans):
        hold_ref[s] = entering
        entering = tot_ref[s] * entering + run_ref[s]
    held = hold_ref[...]
    ends = decay * held + state
    all_ref[...] = ends
    back_ref[:, :sub, :] = keep * jnp.where(block == 0, held, pltpu.roll(ends, 1, 2))
    back_ref[:, sub:, :] = edge_ref[...].reshape(spans, sub, lanes)
    row = lax.broadcasted_iota(jnp.int32, (states, lanes), 0)
    lane = lax.broadcasted_iota(jnp.int32, (states, lanes), 1)
    member = (lane // BLOCKS == row).astype(F32)
    lane_block = lax.broadcasted_iota(jnp.int32, (sub, lanes), 1) % BLOCKS
    for request, _, _, end in laid:
        final = end // steps - 1
        chosen = jnp.where(lane_block == final % BLOCKS, all_ref[final // BLOCKS], 0.0)
        last_ref[request] = lax.dot_general(
            member, chosen, (((1,), (1,)), ((), ())), precision=lax.Precision.HIGHEST, preferred_element_type=F32
        )


def output_kernel(rows, back_ref, delta_ref, drive_ref, rate_ref, coef_ref, act_ref, gate_ref, skip_ref, gated_ref, edge_ref, y_ref):
    span, width = act_ref.shape
    states = rate_ref.shape[0]
    steps = span // BLOCKS
    sources, both, lanes = back_ref.shape
    sub = both // 2
    core = lax.rem(lax.axis_index("chan"), 2)
    edge_ref[...] = jnp.sum(back_ref[:, sub:, :], axis=0)
    start = back_ref[:, :sub, :].reshape(sources * sub, lanes).T
    first = tuple(start[n * BLOCKS : (n + 1) * BLOCKS] for n in range(states))

    def step(t, state):
        now = every(delta_ref, t, steps)
        push = every(drive_ref, t, steps)
        coefs = coef_ref[pl.ds(t, BLOCKS, stride=steps), :]
        moved = []
        total = jnp.zeros((BLOCKS, width), F32)
        for n in range(states):
            after = jnp.exp2(now * rate_ref[n]) * state[n] + push * twice(spread(coefs, n), width)
            total = total + after * twice(spread(coefs, states + n), width)
            moved.append(after)
        for h in range(width // 128):
            y_ref[h, pl.ds(t, BLOCKS, stride=steps), :] = total[:, h * 128 : (h + 1) * 128]
        return tuple(moved)

    lax.fori_loop(0, steps, step, first, unroll=2)
    y = jnp.concatenate([y_ref[h] for h in range(width // 128)], axis=1)
    gated = (y + skip_ref[...] * act_ref[...].astype(F32)) * gate_ref[...]
    even, odd = [], []
    for z in range(span // (2 * rows)):
        even.append(gated[2 * z * rows : (2 * z + 1) * rows])
        odd.append(gated[(2 * z + 1) * rows : (2 * z + 2) * rows])
    even, odd = jnp.concatenate(even, axis=0), jnp.concatenate(odd, axis=0)
    mine = core == 0
    gated_ref[0] = jnp.where(mine, even, odd).astype(BF16)
    gated_ref[1] = jnp.where(mine, odd, even).astype(BF16)


def final_kernel(tokens_ref, parts_ref, out_ref):
    out_ref[...] = (tokens_ref[...].astype(F32) + jnp.sum(parts_ref[...].astype(F32), axis=0)).astype(BF16)


def call(kernel, name, out, *args, scalars=0, scratch=()):
    smem = [pl.BlockSpec(memory_space=pltpu.SMEM)] * scalars
    vmem = pl.BlockSpec(memory_space=pltpu.VMEM)
    shapes = [jax.ShapeDtypeStruct(*o) for o in out]
    result = pl.pallas_call(
        kernel,
        name=name,
        out_shape=shapes,
        in_specs=smem + [vmem] * (len(args) - scalars),
        out_specs=[vmem] * len(out),
        scratch_shapes=list(scratch),
    )(*args)
    return result if len(out) > 1 else result[0]


def on_device(
    tokens,
    norm_gain,
    entry_projection_matrix,
    conv_weight,
    conv_bias,
    w_x,
    timescale_matrix,
    timescale_offset,
    a_log,
    skip_gain,
    w_out,
    lengths,
    req_order,
):
    rows, model = tokens.shape
    chans, spans = lax.axis_size("chan"), lax.axis_size("seq")
    chips = chans // 2
    span = rows * chans
    width = entry_projection_matrix.shape[2]
    states = a_log.shape[0]
    cols = w_x.shape[1]
    reqs, taps = lengths.shape[0], conv_weight.shape[0]
    sub = width // spans
    lanes = states * BLOCKS
    parity = [[2 * z + k for z in range(chips)] for k in range(2)]
    partner = [(i, i ^ 1) for i in range(chans)]
    following = [(i, i + 1) for i in range(spans - 1)]

    def exchange(block, axis, groups=None):
        return lax.all_to_all(block, axis, 0, 0, axis_index_groups=groups)

    copies = call(functools.partial(norm_kernel, chips), "norm", [((chips, rows, model), BF16)], tokens, norm_gain[None])
    own = exchange(copies, "chan", parity).reshape(chips * rows, model)
    other = lax.ppermute(own, "chan", partner)
    own_part = jnp.einsum("td,kde->kte", own, entry_projection_matrix, preferred_element_type=F32)
    inner, gate, tail = call(
        functools.partial(entry_kernel, rows),
        "entry",
        [((span, width), BF16), ((span, width), F32), ((HALO, width), BF16)],
        lengths,
        req_order,
        own_part,
        other,
        entry_projection_matrix,
        scalars=2,
    )
    halo = lax.ppermute(tail, "seq", following)
    activated, part, edge = call(
        conv_kernel,
        "conv",
        [((span, width), BF16), ((span, cols), BF16), ((width, lanes), F32)],
        lengths,
        req_order,
        inner,
        halo,
        conv_weight,
        conv_bias[None],
        w_x,
        scalars=2,
    )
    parts = exchange(part.reshape(chans, rows, cols), "chan")
    summed = call(functools.partial(share_kernel, chans), "share", [((chans, rows, cols), BF16)], parts)
    x_proj = exchange(summed, "chan").reshape(span, cols)
    send, delta, drive, rate, coef = call(
        local_kernel,
        "local",
        [
            ((spans, 2 * sub, lanes), F32),
            ((width // 128, span, 128), F32),
            ((width // 128, span, 128), F32),
            ((states, BLOCKS, width), F32),
            ((span, 128), F32),
        ],
        lengths,
        req_order,
        x_proj,
        timescale_matrix,
        timescale_offset[None],
        activated,
        a_log,
        scalars=2,
    )
    got = exchange(send, "seq")
    back, last_states = call(
        functools.partial(chain_kernel, span // BLOCKS),
        "chain",
        [((spans, 2 * sub, lanes), F32), ((reqs, states, sub), F32)],
        lengths,
        req_order,
        got,
        edge,
        scalars=2,
        scratch=[pltpu.VMEM((spans, sub, lanes), F32)] * 4,
    )
    back = exchange(back, "seq")
    gated, edges = call(
        functools.partial(output_kernel, rows),
        "output",
        [((2, span // 2, width), BF16), ((sub, lanes), F32)],
        back,
        delta,
        drive,
        rate,
        coef,
        activated,
        gate,
        skip_gain[None],
        scratch=[pltpu.VMEM((width // 128, span, 128), F32)],
    )
    theirs = jnp.dot(gated[1], w_out, preferred_element_type=F32).astype(BF16)
    received = lax.ppermute(theirs, "chan", partner)
    ours = jnp.dot(gated[0], w_out, preferred_element_type=F32)
    pair = (ours + received.astype(F32)).astype(BF16).reshape(chips, rows, model)
    mixed = call(final_kernel, "final", [((rows, model), BF16)], tokens, exchange(pair, "chan", parity))
    conv_edges = edges[:, : reqs * taps].T.reshape(reqs, taps, sub).astype(BF16)
    return (mixed, last_states, conv_edges)


def solution(mesh):
    in_specs = (
        P(("seq", "chan"), None),
        P(),
        P(None, None, "chan"),
        P(None, "chan"),
        P("chan"),
        P("chan", None),
        P(None, "chan"),
        P("chan"),
        P(None, "chan"),
        P("chan"),
        P("chan", None),
        P(),
        P(),
    )
    out_specs = (
        P(("seq", "chan"), None),
        P(None, None, ("chan", "seq")),
        P(None, None, ("chan", "seq")),
    )
    return jax.shard_map(
        on_device, mesh=mesh, in_specs=in_specs, out_specs=out_specs, check_vma=False
    )
```

time: 760 us -> 161 us (0.21)
  waiting for transfers between devices: 327 us -> 18.2 us
  starting transfers between devices: 171 us -> 16.2 us
  other arithmetic: 52.1 us -> 0.01 us
  blocking collectives: 142 us -> 92.2 us
  local copies, waits for them, and re-layouts: 38.7 us -> 4.33 us
  Pallas kernels: 0 us -> 22.6 us
  between operations: 14.9 us -> 0.72 us
    ppermute x32 -> x3, starting transfers between devices: 171 us -> 12.7 us  [the longest x1 5.4 us: on_device(): received = lax.ppermute(theirs, 'chan', partner)]
    unnamed x1 -> x0, blocking collectives: 142 us -> none
    psum x1 -> x0, waiting for transfers between devices: 109 us -> none  [on_device(): lax.psum(jnp.dot(activated, w_x, preferred_element_type=jnp.float32), 'ch...]
    all_to_all x0 -> x5, blocking collectives: none -> 92.2 us  [exchange(): return lax.all_to_all(block, axis, 0, 0, axis_index_groups=groups)]
    unnamed x5 -> x0, waiting for transfers between devices: 84.2 us -> none
    reduce_scatter x1 -> x0, waiting for transfers between devices: 64 us -> none  [on_device(): lax.psum_scatter(jnp.dot(switched_result, w_out, preferred_element_type=j...]
    all_gather x1 -> x0, waiting for transfers between devices: 43.6 us -> none  [on_device(): lax.all_gather(rescaled_entries, 'chan', axis=0, tiled=True)]
    ppermute x32 -> x3, waiting for transfers between devices: 26.3 us -> 1.69 us  [the longest x1 1.51 us: on_device(): received = lax.ppermute(theirs, 'chan', partner)]
  transfers between devices with their start and end apart: 36 -> 4, of which waited for: 35 -> 3; matrix products, arithmetic and copies ran while one was open for 2% -> 3% of each run, Pallas kernels for 0% -> 0%
where the time goes in v1:
time: 161 us; the launch traced here: 160 us
  blocking collectives  92.2 us (57%)
  Pallas kernels  22.6 us (14%)
  waiting for transfers between devices  18.2 us (11%)
  starting transfers between devices  16.2 us (10%)
  matrix products  5.85 us (4%)
  local copies, waits for them, and re-layouts  4.33 us (3%)
    all_to_all x5, blocking collectives, exchange(): return lax.all_to_all(block, axis, 0, 0, axis_index_groups=groups)  92.2 us
    pallas_call x8, Pallas kernels, call(): pl.pallas_call(kernel, name=name, out_shape=shapes, in_specs=smem + [vmem...  22.6 us
    all_to_all x1, waiting for transfers between devices, exchange(): return lax.all_to_all(block, axis, 0, 0, axis_index_groups=groups)  16.5 us
    ppermute x1, starting transfers between devices, on_device(): received = lax.ppermute(theirs, 'chan', partner)  5.4 us
    ppermute x1, starting transfers between devices, on_device(): other = lax.ppermute(own, 'chan', partner)  4.23 us
    unnamed x16, local copies, waits for them, and re-layouts  3.65 us
    all_to_all x1, starting transfers between devices, exchange(): return lax.all_to_all(block, axis, 0, 0, axis_index_groups=groups)  3.49 us
  transfers between devices with their start and end apart: 4, of which 3 were waited for; matrix products, arithmetic and copies ran while one was open for 3% of the time, Pallas kernels for 0%

profile of v1, /device:TPU:1, one launch (start us, length us, event | category | flops | bytes accessed | tf_op | source)
XLA Modules:
  0.0 160.1 jit_solution(125413512891572004)
XLA Ops:
  0.6 0.0 copy-start
  0.6 1.9 %norm.1 = bf16[8,16,2048]{2,1,0:T(8,128)(2,1)} custom-call(bf16[16,2048]{1,0:T(8,128)(2,1)} %tokens_ref.3, f32[1,2048]{1,0:T(1,128)} %bitcast.31), custom_call_target="tpu_custom_call" | custom-call | tf_op jit(solution)/shard_map/norm/pallas_call | solution.py:266
  2.5 27.0 %all_to_all.30 = bf16[8,16,2048]{2,1,0:T(8,128)(2,1)S(1)} all-to-all(bf16[8,16,2048]{2,1,0:T(8,128)(2,1)} %norm.1), channel_id=1, replica_groups={{0,2,4,6,8,10,12,14},{1,3,5,7,9,11,13,15},{16,18,20,22,24,26,28,30},{17..., dimensions={0} | all-to-all | bytes 1048576 | tf_op jit(solution)/shard_map/all_to_all | solution.py:307
  29.5 4.2 %collective-permute-start = (bf16[128,2048]{1,0:T(8,128)(2,1)S(1)}, bf16[128,2048]{1,0:T(8,128)(2,1)S(1)}, u32[]{:S(2)}, u32[]{:S(2)}) collective-permute-start(bf16[128,2048]{1,0:T(8,128)(2,1)S(1)} %bitcast.27), channel_id=1, source_target_pairs={{0,1},{1,0},{2,3},{3,2},{4,5},{5,4},{6,7},{7,6},{8,9},{9,8},{10,11... | collective-permute-start | bytes 1572872 | tf_op jit(solution)/shard_map/ppermute | solution.py:311
  33.7 2.7 %convolution_bitcast_fusion.own_ref = f32[2,128,256]{2,1,0:T(8,128)} fusion(bf16[128,2048,1]{1,0,2:T(8,128)(2,1)S(1)} %bitcast.28, bf16[2,2048,256]{2,1,0:T(8,128)(2,1)} %weight_ref.1), kind=kOutput, calls=%fused_computation.1 | convolution fusion | flops 268435456 | bytes 2883584 | tf_op jit(solution)/shard_map/td,kde->kte/dot_general | solution.py:312
  36.5 0.0 copy-start.3
  36.5 0.0 collective-permute-done.other_ref
  36.5 0.0 copy-start.2
  36.5 0.8 copy-done.2
  37.3 3.2 %entry.1 = (bf16[256,256]{1,0:T(8,128)(2,1)}, f32[256,256]{1,0:T(8,128)}, bf16[8,256]{1,0:T(8,128)(2,1)}) custom-call(s32[4]{0:T(128)} %lengths_ref.7, s32[4]{0:T(128)} %order_ref.7, f32[2,128,256]{2,1,0:T(8,128)} %convolution_bitcast_fusion.own_ref, bf16[128,2048]{1,0:T(8,128)(2,1)} %copy-done.2, bf16[2,2048,256]{2,1,0:T(8,128)(2,1)} %weight_ref.1), custom_call_target="tpu_custom_call" | custom-call | tf_op jit(solution)/shard_map/entry/pallas_call | solution.py:266
  40.4 3.1 %collective-permute-start.1 = (bf16[8,256]{1,0:T(8,128)(2,1)}, bf16[8,256]{1,0:T(8,128)(2,1)S(1)}, u32[]{:S(2)}, u32[]{:S(2)}) collective-permute-start(bf16[8,256]{1,0:T(8,128)(2,1)} %get-tuple-element.19), channel_id=1, source_target_pairs={{0,16},{16,32},{32,48},{48,64},{64,80},{80,96},{96,112},{112,128},... | collective-permute-start | bytes 12296 | tf_op jit(solution)/shard_map/ppermute | solution.py:324
  43.5 0.0 copy-done.3
  43.5 0.8 copy.16.wx_ref
  44.3 0.2 collective-permute-done.1.halo_ref
  44.5 0.0 copy-start.5
  44.5 0.6 copy-done.5
  45.1 2.1 %conv.1 = (bf16[256,256]{1,0:T(8,128)(2,1)}, bf16[256,160]{1,0:T(8,128)(2,1)}, f32[256,128]{1,0:T(8,128)}) custom-call(s32[4]{0:T(128)} %lengths_ref.7, s32[4]{0:T(128)} %order_ref.7, bf16[256,256]{1,0:T(8,128)(2,1)} %get-tuple-element.18.inner_ref, bf16[8,256]{1,0:T(8,128)(2,1)} %copy-done.5, f32[4,256]{1,0:T(4,128)} %taps_ref.1, f32[1,256]{1,0:T(1,128)} %bitcast.33, ...), custom_call_target="tpu_custom_call" | custom-call | tf_op jit(solution)/shard_map/conv/pallas_call | solution.py:266
  47.2 14.0 %all_to_all.31.parts_ref = bf16[16,16,160]{2,1,0:T(8,128)(2,1)} all-to-all(bf16[16,16,160]{2,1,0:T(8,128)(2,1)} %bitcast.30), channel_id=1, replica_groups=mesh['seq'=32,'chan'=16] {'chan'}, dimensions={0} | all-to-all | bytes 163840 | tf_op jit(solution)/shard_map/all_to_all | solution.py:307
  61.2 1.6 share.1
  62.8 12.5 %all_to_all.32 = bf16[16,16,160]{2,1,0:T(8,128)(2,1)} all-to-all(bf16[16,16,160]{2,1,0:T(8,128)(2,1)} %share.1), channel_id=1, replica_groups=mesh['seq'=32,'chan'=16] {'chan'}, dimensions={0} | all-to-all | bytes 163840 | tf_op jit(solution)/shard_map/all_to_all | solution.py:307
  75.4 4.4 %local.1 = (f32[32,16,128]{2,1,0:T(8,128)}, f32[2,256,128]{2,1,0:T(8,128)}, f32[2,256,128]{2,1,0:T(8,128)}, f32[16,8,256]{2,1,0:T(8,128)}, f32[256,128]{1,0:T(8,128)}) custom-call(s32[4]{0:T(128)} %lengths_ref.7, s32[4]{0:T(128)} %order_ref.7, bf16[256,160]{1,0:T(8,128)(2,1)} %bitcast.29, bf16[128,256]{1,0:T(8,128)(2,1)} %tm_ref.1, f32[1,256]{1,0:T(1,128)} %bitcast.34, ...), custom_call_target="tpu_custom_call" | custom-call | tf_op jit(solution)/shard_map/local/pallas_call | solution.py:266
  79.8 23.6 %all_to_all.33.got_ref = f32[32,16,128]{2,1,0:T(8,128)} all-to-all(f32[32,16,128]{2,1,0:T(8,128)} %get-tuple-element.22), channel_id=1, replica_groups=mesh['seq'=32,'chan'=16] {'seq'}, dimensions={0} | all-to-all | bytes 524288 | tf_op jit(solution)/shard_map/all_to_all | solution.py:307
  103.3 2.4 %chain.1 = (f32[32,16,128]{2,1,0:T(8,128)}, f32[4,16,8]{2,1,0:T(8,128)}) custom-call(s32[4]{0:T(128)} %lengths_ref.7, s32[4]{0:T(128)} %order_ref.7, f32[32,16,128]{2,1,0:T(8,128)} %all_to_all.33.got_ref, f32[256,128]{1,0:T(8,128)} %get-tuple-element.23.edge_ref), custom_call_target="tpu_custom_call" | custom-call | tf_op jit(solution)/shard_map/chain/pallas_call | solution.py:266
  105.7 15.1 %all_to_all.34.back_ref = f32[32,16,128]{2,1,0:T(8,128)} all-to-all(f32[32,16,128]{2,1,0:T(8,128)} %get-tuple-element.24), channel_id=1, replica_groups=mesh['seq'=32,'chan'=16] {'seq'}, dimensions={0} | all-to-all | bytes 524288 | tf_op jit(solution)/shard_map/all_to_all | solution.py:307
  120.9 5.3 %output.1 = (bf16[2,128,256]{2,1,0:T(8,128)(2,1)}, f32[8,128]{1,0:T(8,128)}) custom-call(f32[32,16,128]{2,1,0:T(8,128)} %all_to_all.34.back_ref, f32[2,256,128]{2,1,0:T(8,128)} %get-tuple-element.25.delta_ref, f32[2,256,128]{2,1,0:T(8,128)} %get-tuple-element.26.drive_ref, f32[16,8,256]{2,1,0:T(8,128)} %get-tuple-element.27.rate_ref, ...), custom_call_target="tpu_custom_call" | custom-call | tf_op jit(solution)/shard_map/output/pallas_call | solution.py:266
  126.1 0.0 copy-done
  126.1 0.0 copy-start.4
  126.1 0.0 copy-start.6
  126.1 1.2 convolution_convert_fusion
  127.3 5.4 %collective-permute-start.2 = (bf16[128,2048]{1,0:T(8,128)(2,1)S(1)}, bf16[128,2048]{1,0:T(8,128)(2,1)S(1)}, u32[]{:S(2)}, u32[]{:S(2)}) collective-permute-start(bf16[128,2048]{1,0:T(8,128)(2,1)S(1)} %convolution_convert_fusion), channel_id=1, source_target_pairs={{0,1},{1,0},{2,3},{3,2},{4,5},{5,4},{6,7},{7,6},{8,9},{9,8},{10,11... | collective-permute-start | bytes 1572872 | tf_op jit(solution)/shard_map/ppermute | solution.py:388
  132.7 1.5 collective-permute-done.2
  134.2 1.9 %add_convert_fusion = bf16[128,2048]{1,0:T(8,128)(2,1)} fusion(bf16[128,2048]{1,0:T(8,128)(2,1)S(1)} %collective-permute-done.2, bf16[256,2048]{1,0:T(8,128)(2,1)S(1)} %copy-done, bf16[2,128,256]{2,1,0:T(8,128)(2,1)} %get-tuple-element.30), kind=kOutput, calls=%fused_computation.2 | convolution fusion | flops 135004160 | bytes 2162688 | tf_op jit(solution)/shard_map/dot_general | solution.py:389
  136.2 3.5 %all-to-all-start.5 = ((bf16[8,16,2048]{2,1,0:T(8,128)(2,1)}), bf16[8,16,2048]{2,1,0:T(8,128)(2,1)S(1)}, u32[]{:S(2)}, u32[]{:S(2)}) async-start(bf16[8,16,2048]{2,1,0:T(8,128)(2,1)} %bitcast.11), calls=%async_computation.5 | async-start | bytes 1048576 | tf_op jit(solution)/shard_map/all_to_all | solution.py:307
  139.7 0.0 copy-done.4
  139.7 0.7 copy.18
  140.4 0.0 copy-done.6
  140.4 0.7 copy.17
  141.0 16.5 %all-to-all-done.5.parts_ref = bf16[8,16,2048]{2,1,0:T(8,128)(2,1)S(1)} async-done(((bf16[8,16,2048]{2,1,0:T(8,128)(2,1)}), bf16[8,16,2048]{2,1,0:T(8,128)(2,1)S(1)}, u32[]{:S(2)}, u32[]{:S(2)}) %all-to-all-start.5) | async-done | bytes 524320 | tf_op jit(solution)/shard_map/all_to_all | solution.py:307
  157.6 0.0 copy-start.1
  157.6 0.8 copy-done.1
  158.3 1.8 %final.1 = bf16[16,2048]{1,0:T(8,128)(2,1)} custom-call(bf16[16,2048]{1,0:T(8,128)(2,1)} %tokens_ref.3, bf16[8,16,2048]{2,1,0:T(8,128)(2,1)} %copy-done.1), custom_call_target="tpu_custom_call" | custom-call | tf_op jit(solution)/shard_map/final/pallas_call | solution.py:266
  (2 shorter events, 0.0 us)
Async XLA Ops:
  0.6 125.5 %copy-start = (bf16[256,2048]{1,0:T(8,128)(2,1)S(1)}, bf16[256,2048]{1,0:T(8,128)(2,1)}, u32[]{:S(2)}) copy-start(bf16[256,2048]{1,0:T(8,128)(2,1)} %param.23) | copy-start | bytes 3145732
  29.5 7.0 %collective-permute-start = (bf16[128,2048]{1,0:T(8,128)(2,1)S(1)}, bf16[128,2048]{1,0:T(8,128)(2,1)S(1)}, u32[]{:S(2)}, u32[]{:S(2)}) collective-permute-start(bf16[128,2048]{1,0:T(8,128)(2,1)S(1)} %bitcast.27), channel_id=1, source_target_pairs={{0,1},{1,0},{2,3},{3,2},{4,5},{5,4},{6,7},{7,6},{8,9},{9,8},{10,11... | collective-permute-start | bytes 1572872 | tf_op jit(solution)/shard_map/ppermute | solution.py:311
  36.5 7.1 %copy-start.3 = (bf16[256,160]{0,1:T(8,128)(2,1)S(1)}, bf16[256,160]{0,1:T(8,128)(2,1)}, u32[]{:S(2)}) copy-start(bf16[256,160]{0,1:T(8,128)(2,1)} %param.18) | copy-start | bytes 245764
  36.5 0.8 copy-start.2
  40.4 4.1 %collective-permute-start.1 = (bf16[8,256]{1,0:T(8,128)(2,1)}, bf16[8,256]{1,0:T(8,128)(2,1)S(1)}, u32[]{:S(2)}, u32[]{:S(2)}) collective-permute-start(bf16[8,256]{1,0:T(8,128)(2,1)} %get-tuple-element.19), channel_id=1, source_target_pairs={{0,16},{16,32},{32,48},{48,64},{64,80},{80,96},{96,112},{112,128},... | collective-permute-start | bytes 12296 | tf_op jit(solution)/shard_map/ppermute | solution.py:324
  44.5 0.6 copy-start.5
  126.1 13.6 %copy-start.4 = (f32[4,16,8]{2,1,0:T(8,128)S(1)}, f32[4,16,8]{2,1,0:T(8,128)}, u32[]{:S(2)}) copy-start(f32[4,16,8]{2,1,0:T(8,128)} %get-tuple-element.34) | copy-start | bytes 6148
  126.1 14.2 %copy-start.6 = (f32[8,128]{1,0:T(8,128)S(1)}, f32[8,128]{1,0:T(8,128)}, u32[]{:S(2)}) copy-start(f32[8,128]{1,0:T(8,128)} %get-tuple-element.32) | copy-start | bytes 12292
  127.3 6.9 %collective-permute-start.2 = (bf16[128,2048]{1,0:T(8,128)(2,1)S(1)}, bf16[128,2048]{1,0:T(8,128)(2,1)S(1)}, u32[]{:S(2)}, u32[]{:S(2)}) collective-permute-start(bf16[128,2048]{1,0:T(8,128)(2,1)S(1)} %convolution_convert_fusion), channel_id=1, source_target_pairs={{0,1},{1,0},{2,3},{3,2},{4,5},{5,4},{6,7},{7,6},{8,9},{9,8},{10,11... | collective-permute-start | bytes 1572872 | tf_op jit(solution)/shard_map/ppermute | solution.py:388
  136.2 21.4 %all-to-all-start.5 = ((bf16[8,16,2048]{2,1,0:T(8,128)(2,1)}), bf16[8,16,2048]{2,1,0:T(8,128)(2,1)S(1)}, u32[]{:S(2)}, u32[]{:S(2)}) async-start(bf16[8,16,2048]{2,1,0:T(8,128)(2,1)} %bitcast.11), calls=%async_computation.5 | async-start | bytes 1048576 | tf_op jit(solution)/shard_map/all_to_all | solution.py:307
  157.6 0.8 copy-start.1

commit v2 on v1

--- a/solution.py
+++ b/solution.py
@@ -13,6 +13,7 @@
 F32 = jnp.float32
 BF16 = jnp.bfloat16
 HALO = 8
+GRANT = 16 << 20
 
 
 def placements(lengths_ref, order_ref):
@@ -93,7 +94,9 @@
             total = total + taps_ref[k : k + 1, :] * extended[shift : shift + STRETCH]
         act_ref[pl.ds(q * STRETCH, STRETCH), :] = (total / (1.0 + jnp.exp(-total))).astype(BF16)
         before = here[STRETCH - HALO :]
-    part_ref[...] = jnp.dot(act_ref[...], wx_ref[...], preferred_element_type=F32).astype(BF16)
+    part_ref[...] = lax.dot_general(
+        act_ref[...], wx_ref[...], (((1,), (1,)), ((), ())), preferred_element_type=F32
+    ).astype(BF16)
     column = lax.broadcasted_iota(jnp.int32, (1, 128), 1)
     target = jnp.full((1, 128), -1, jnp.int32)
     for request, begin, length, _ in laid:
@@ -102,7 +105,8 @@
         target = jnp.where(mine, begin + back, target)
     slots = base + lax.broadcasted_iota(jnp.int32, (span, 128), 0)
     pick = (slots == target).astype(F32).astype(BF16)
-    edge_ref[...] = lax.dot_general(inner, pick, (((0,), (0,)), ((), ())), preferred_element_type=F32)
+    edges = lax.dot_general(inner, pick, (((0,), (0,)), ((), ())), preferred_element_type=F32)
+    edge_ref[...] = edges.astype(BF16)
 
 
 def share_kernel(copies, parts_ref, out_ref):
@@ -160,14 +164,19 @@
 
     zero = jnp.zeros((BLOCKS, width), F32)
     total, state = lax.fori_loop(0, steps, step, (zero, (zero,) * states), unroll=2)
-    dests, both, _ = send_ref.shape
+    dests, both, lanes = send_ref.shape
     sub = both // 2
-    send_ref[:, :sub, :] = jnp.concatenate(state, axis=0).T.reshape(dests, sub, states * BLOCKS)
-    decay = [jnp.exp2(total * rate_ref[n]) for n in range(states)]
-    send_ref[:, sub:, :] = jnp.concatenate(decay, axis=0).T.reshape(dests, sub, states * BLOCKS)
-
-
-def chain_kernel(steps, lengths_ref, order_ref, got_ref, edge_ref, back_ref, last_ref, run_ref, tot_ref, all_ref, hold_ref):
+    send_ref[:, :sub, :] = jnp.concatenate(state, axis=0).T.reshape(dests, sub, lanes).astype(BF16)
+    terms = []
+    for _ in range(3):
+        term = total.astype(BF16).astype(F32)
+        terms.append(term)
+        total = total - term
+    terms.append(jnp.zeros((lanes - 3 * BLOCKS, width), F32))
+    send_ref[:, sub:, :] = jnp.concatenate(terms, axis=0).T.reshape(dests, sub, lanes).astype(BF16)
+
+
+def chain_kernel(steps, lengths_ref, order_ref, got_ref, edge_ref, alog_ref, back_ref, last_ref, rate_ref, run_ref, tot_ref, all_ref, hold_ref):
     spans, both, lanes = got_ref.shape
     sub = both // 2
     states = lanes // BLOCKS
@@ -175,8 +184,20 @@
     block = lax.broadcasted_iota(jnp.int32, (1, 1, lanes), 2) % BLOCKS
     index = lax.broadcasted_iota(jnp.int32, (spans, 1, lanes), 0) * BLOCKS + block
     keep = jnp.where(opens(laid, index * steps), 0.0, 1.0)
-    state = got_ref[:, :sub, :]
-    decay = got_ref[:, sub:, :] * keep
+    row = lax.broadcasted_iota(jnp.int32, (states, lanes), 0)
+    lane = lax.broadcasted_iota(jnp.int32, (states, lanes), 1)
+    member = (lane // BLOCKS == row).astype(F32)
+    rate = -jnp.exp(alog_ref[...]) * LOG2E
+    rate_ref[...] = lax.dot_general(
+        rate, member, (((0,), (0,)), ((), ())), precision=lax.Precision.HIGHEST, preferred_element_type=F32
+    )
+    mine = rate_ref[pl.ds(pl.multiple_of(lax.axis_index("seq") * sub, sub), sub), :]
+    source = lax.broadcasted_iota(jnp.int32, (lanes, lanes), 0)
+    target = lax.broadcasted_iota(jnp.int32, (lanes, lanes), 1)
+    gather = ((source % BLOCKS == target % BLOCKS) & (source < 3 * BLOCKS)).astype(F32).astype(BF16)
+    sums = jnp.dot(got_ref[:, sub:, :].reshape(spans * sub, lanes), gather, preferred_element_type=F32)
+    state = got_ref[:, :sub, :].astype(F32)
+    decay = jnp.exp2(sums.reshape(spans, sub, lanes) * mine[None]) * keep
     shift = 1
     while shift < BLOCKS:
         within = block >= shift
@@ -203,29 +224,26 @@
     held = hold_ref[...]
     ends = decay * held + state
     all_ref[...] = ends
-    back_ref[:, :sub, :] = keep * jnp.where(block == 0, held, pltpu.roll(ends, 1, 2))
+    back_ref[:, :sub, :] = (keep * jnp.where(block == 0, held, pltpu.roll(ends, 1, 2))).astype(BF16)
     back_ref[:, sub:, :] = edge_ref[...].reshape(spans, sub, lanes)
-    row = lax.broadcasted_iota(jnp.int32, (states, lanes), 0)
-    lane = lax.broadcasted_iota(jnp.int32, (states, lanes), 1)
-    member = (lane // BLOCKS == row).astype(F32)
     lane_block = lax.broadcasted_iota(jnp.int32, (sub, lanes), 1) % BLOCKS
     for request, _, _, end in laid:
         final = end // steps - 1
         chosen = jnp.where(lane_block == final % BLOCKS, all_ref[final // BLOCKS], 0.0)
         last_ref[request] = lax.dot_general(
-            member, chosen, (((1,), (1,)), ((), ())), precision=lax.Precision.HIGHEST, preferred_element_type=F32
+            chosen, member, (((1,), (1,)), ((), ())), precision=lax.Precision.HIGHEST, preferred_element_type=F32
         )
 
 
-def output_kernel(rows, back_ref, delta_ref, drive_ref, rate_ref, coef_ref, act_ref, gate_ref, skip_ref, gated_ref, edge_ref, y_ref):
+def output_kernel(rows, back_ref, delta_ref, drive_ref, rate_ref, coef_ref, act_ref, gate_ref, skip_ref, wout_ref, gated_ref, theirs_ref, edge_ref, y_ref):
     span, width = act_ref.shape
     states = rate_ref.shape[0]
     steps = span // BLOCKS
     sources, both, lanes = back_ref.shape
     sub = both // 2
     core = lax.rem(lax.axis_index("chan"), 2)
-    edge_ref[...] = jnp.sum(back_ref[:, sub:, :], axis=0)
-    start = back_ref[:, :sub, :].reshape(sources * sub, lanes).T
+    edge_ref[...] = jnp.sum(back_ref[:, sub:, :].astype(F32), axis=0)
+    start = back_ref[:, :sub, :].astype(F32).reshape(sources * sub, lanes).T
     first = tuple(start[n * BLOCKS : (n + 1) * BLOCKS] for n in range(states))
 
     def step(t, state):
@@ -251,8 +269,9 @@
         odd.append(gated[(2 * z + 1) * rows : (2 * z + 2) * rows])
     even, odd = jnp.concatenate(even, axis=0), jnp.concatenate(odd, axis=0)
     mine = core == 0
-    gated_ref[0] = jnp.where(mine, even, odd).astype(BF16)
-    gated_ref[1] = jnp.where(mine, odd, even).astype(BF16)
+    gated_ref[...] = jnp.where(mine, even, odd).astype(BF16)
+    away = jnp.where(mine, odd, even).astype(BF16)
+    theirs_ref[...] = jnp.dot(away, wout_ref[...], preferred_element_type=F32).astype(BF16)
 
 
 def final_kernel(tokens_ref, parts_ref, out_ref):
@@ -262,7 +281,8 @@
 def call(kernel, name, out, *args, scalars=0, scratch=()):
     smem = [pl.BlockSpec(memory_space=pltpu.SMEM)] * scalars
     vmem = pl.BlockSpec(memory_space=pltpu.VMEM)
-    shapes = [jax.ShapeDtypeStruct(*o) for o in out]
+    shapes = [jax.ShapeDtypeStruct(*o) if name == "final" else pltpu.VMEM(*o) for o in out]
+    args = args[:scalars] + tuple(pltpu.with_memory_space_constraint(a, pltpu.VMEM) for a in args[scalars:])
     result = pl.pallas_call(
         kernel,
         name=name,
@@ -270,6 +290,7 @@
         in_specs=smem + [vmem] * (len(args) - scalars),
         out_specs=[vmem] * len(out),
         scratch_shapes=list(scratch),
+        compiler_params=pltpu.CompilerParams(vmem_limit_bytes=GRANT),
     )(*args)
     return result if len(out) > 1 else result[0]
 
@@ -325,14 +346,14 @@
     activated, part, edge = call(
         conv_kernel,
         "conv",
-        [((span, width), BF16), ((span, cols), BF16), ((width, lanes), F32)],
+        [((span, width), BF16), ((span, cols), BF16), ((width, lanes), BF16)],
         lengths,
         req_order,
         inner,
         halo,
         conv_weight,
         conv_bias[None],
-        w_x,
+        w_x.T,
         scalars=2,
     )
     parts = exchange(part.reshape(chans, rows, cols), "chan")
@@ -342,7 +363,7 @@
         local_kernel,
         "local",
         [
-            ((spans, 2 * sub, lanes), F32),
+            ((spans, 2 * sub, lanes), BF16),
             ((width // 128, span, 128), F32),
             ((width // 128, span, 128), F32),
             ((states, BLOCKS, width), F32),
@@ -361,19 +382,20 @@
     back, last_states = call(
         functools.partial(chain_kernel, span // BLOCKS),
         "chain",
-        [((spans, 2 * sub, lanes), F32), ((reqs, states, sub), F32)],
+        [((spans, 2 * sub, lanes), BF16), ((reqs, sub, states), F32)],
         lengths,
         req_order,
         got,
         edge,
+        a_log,
         scalars=2,
-        scratch=[pltpu.VMEM((spans, sub, lanes), F32)] * 4,
+        scratch=[pltpu.VMEM((width, lanes), F32)] + [pltpu.VMEM((spans, sub, lanes), F32)] * 4,
     )
     back = exchange(back, "seq")
-    gated, edges = call(
+    gated, theirs, edges = call(
         functools.partial(output_kernel, rows),
         "output",
-        [((2, span // 2, width), BF16), ((sub, lanes), F32)],
+        [((span // 2, width), BF16), ((span // 2, model), BF16), ((sub, lanes), F32)],
         back,
         delta,
         drive,
@@ -382,15 +404,15 @@
         activated,
         gate,
         skip_gain[None],
+        w_out,
         scratch=[pltpu.VMEM((width // 128, span, 128), F32)],
     )
-    theirs = jnp.dot(gated[1], w_out, preferred_element_type=F32).astype(BF16)
     received = lax.ppermute(theirs, "chan", partner)
-    ours = jnp.dot(gated[0], w_out, preferred_element_type=F32)
+    ours = lax.optimization_barrier(jnp.dot(gated, w_out, preferred_element_type=F32))
     pair = (ours + received.astype(F32)).astype(BF16).reshape(chips, rows, model)
     mixed = call(final_kernel, "final", [((rows, model), BF16)], tokens, exchange(pair, "chan", parity))
     conv_edges = edges[:, : reqs * taps].T.reshape(reqs, taps, sub).astype(BF16)
-    return (mixed, last_states, conv_edges)
+    return (mixed, jnp.swapaxes(last_states, 1, 2), conv_edges)
 
 
 def solution(mesh):

time: 161 us -> 137 us (0.85)
  Pallas kernels: 22.6 us -> 11.3 us
  blocking collectives: 92.2 us -> 84.4 us
  matrix products: 5.85 us -> 2.34 us
    pallas_call x8, Pallas kernels: 22.6 us -> 11.3 us  [call(): pl.pallas_call(kernel, name=name, out_shape=shapes, in_specs=smem + [vmem...]
    all_to_all x5, blocking collectives: 92.2 us -> 84.4 us  [exchange(): return lax.all_to_all(block, axis, 0, 0, axis_index_groups=groups)]
    dot_general x2 -> x1, matrix products: 3.11 us -> 0.31 us  [on_device(): jnp.dot(gated, w_out, preferred_element_type=F32)]
    unnamed x16 -> x29, local copies, waits for them, and re-layouts: 3.65 us -> 2.21 us
where the time goes in v2:
time: 137 us
  blocking collectives  84.4 us (62%)
  waiting for transfers between devices  18.5 us (14%)
  starting transfers between devices  15.4 us (11%)
  Pallas kernels  11.3 us (8%)
  local copies, waits for them, and re-layouts  2.89 us (2%)
  matrix products  2.34 us (2%)
    all_to_all x5, blocking collectives, exchange(): return lax.all_to_all(block, axis, 0, 0, axis_index_groups=groups)  84.4 us
    all_to_all x1, waiting for transfers between devices, exchange(): return lax.all_to_all(block, axis, 0, 0, axis_index_groups=groups)  16.6 us
    pallas_call x8, Pallas kernels, call(): pl.pallas_call(kernel, name=name, out_shape=shapes, in_specs=smem + [vmem...  11.3 us
    ppermute x1, starting transfers between devices, on_device(): received = lax.ppermute(theirs, 'chan', partner)  4.55 us
    ppermute x1, starting transfers between devices, on_device(): other = lax.ppermute(own, 'chan', partner)  4.23 us
    all_to_all x1, starting transfers between devices, exchange(): return lax.all_to_all(block, axis, 0, 0, axis_index_groups=groups)  3.49 us
    ppermute x1, starting transfers between devices, on_device(): halo = lax.ppermute(tail, 'seq', following)  3.1 us
  transfers between devices with their start and end apart: 4, of which 3 were waited for; matrix products, arithmetic and copies ran while one was open for 3% of the time, Pallas kernels for 0%

profile of v2, /device:TPU:1, one launch (start us, length us, event | category | flops | bytes accessed | tf_op | source)
XLA Modules:
  0.0 136.7 jit_solution(6655134032026881067)
XLA Ops:
  0.6 0.0 copy-start.2
  0.6 0.8 copy-done.2
  1.5 0.0 copy-start.7
  1.5 0.7 copy-done.7
  2.2 0.1 norm.1
  2.3 0.0 copy-start
  2.3 0.0 copy-start.8
  2.3 0.0 copy-start.9
  2.4 26.9 %all_to_all.30 = bf16[8,16,2048]{2,1,0:T(8,128)(2,1)S(1)} all-to-all(bf16[8,16,2048]{2,1,0:T(8,128)(2,1)S(1)} %norm.1), channel_id=1, replica_groups={{0,2,4,6,8,10,12,14},{1,3,5,7,9,11,13,15},{16,18,20,22,24,26,28,30},{17..., dimensions={0} | all-to-all | bytes 1048576 | tf_op jit(solution)/shard_map/all_to_all | solution.py:328
  29.2 4.2 %collective-permute-start = (bf16[128,2048]{1,0:T(8,128)(2,1)S(1)}, bf16[128,2048]{1,0:T(8,128)(2,1)S(1)}, u32[]{:S(2)}, u32[]{:S(2)}) collective-permute-start(bf16[128,2048]{1,0:T(8,128)(2,1)S(1)} %bitcast.29), channel_id=1, source_target_pairs={{0,1},{1,0},{2,3},{3,2},{4,5},{5,4},{6,7},{7,6},{8,9},{9,8},{10,11... | collective-permute-start | bytes 1572872 | tf_op jit(solution)/shard_map/ppermute | solution.py:332
  33.5 2.0 %convolution_bitcast_fusion.own_ref = f32[2,128,256]{2,1,0:T(8,128)S(1)} fusion(bf16[128,2048,1]{1,0,2:T(8,128)(2,1)S(1)} %bitcast.30, bf16[2,2048,256]{2,1,0:T(8,128)(2,1)} %weight_ref.1), kind=kOutput, calls=%fused_computation | convolution fusion | flops 268435456 | bytes 2883584 | tf_op jit(solution)/shard_map/td,kde->kte/dot_general | solution.py:333
  35.5 0.0 copy-start.4
  35.5 0.0 copy-start.10
  35.5 0.0 copy-start.11
  35.6 0.0 copy-start.5
  35.6 0.0 copy-start.6
  35.6 0.0 copy-start.12
  35.6 0.0 copy-start.1
  35.6 0.0 copy-start.13
  35.6 0.0 collective-permute-done.other_ref
  35.6 0.0 copy-done
  35.6 0.0 copy-done.8
  35.7 0.0 copy-done.9
  35.7 1.1 entry.1
  36.8 3.1 %collective-permute-start.1 = (bf16[8,256]{1,0:T(8,128)(2,1)S(1)}, bf16[8,256]{1,0:T(8,128)(2,1)S(1)}, u32[]{:S(2)}, u32[]{:S(2)}) collective-permute-start(bf16[8,256]{1,0:T(8,128)(2,1)S(1)} %get-tuple-element.20), channel_id=1, source_target_pairs={{0,16},{16,32},{32,48},{48,64},{64,80},{80,96},{96,112},{112,128},... | collective-permute-start | bytes 12296 | tf_op jit(solution)/shard_map/ppermute | solution.py:345
  39.9 0.7 collective-permute-done.1.halo_ref
  40.6 0.0 copy-done.4
  40.6 0.0 copy-done.10
  40.6 0.0 copy-done.11
  40.6 1.0 conv.1
  41.6 12.5 %all_to_all.31.parts_ref = bf16[16,16,160]{2,1,0:T(8,128)(2,1)S(1)} all-to-all(bf16[16,16,160]{2,1,0:T(8,128)(2,1)S(1)} %bitcast.23), channel_id=1, replica_groups=mesh['seq'=32,'chan'=16] {'chan'}, dimensions={0} | all-to-all | bytes 163840 | tf_op jit(solution)/shard_map/all_to_all | solution.py:328
  54.1 11.3 %all_to_all.32 = bf16[16,16,160]{2,1,0:T(8,128)(2,1)S(1)} all-to-all(bf16[16,16,160]{2,1,0:T(8,128)(2,1)S(1)} %share.1), channel_id=1, replica_groups=mesh['seq'=32,'chan'=16] {'chan'}, dimensions={0} | all-to-all | bytes 163840 | tf_op jit(solution)/shard_map/all_to_all | solution.py:328
  65.4 0.0 copy-done.5
  65.4 0.0 copy-done.6
  65.4 0.0 copy-done.12
  65.4 3.1 %local.1 = (bf16[32,16,128]{2,1,0:T(8,128)(2,1)S(1)}, f32[2,256,128]{2,1,0:T(8,128)S(1)}, f32[2,256,128]{2,1,0:T(8,128)S(1)}, f32[16,8,256]{2,1,0:T(8,128)S(1)}, f32[256,128]{1,0:T(8,128)S(1)}) custom-call(s32[4]{0:T(128)S(1)} %copy-done.8, s32[4]{0:T(128)S(1)} %copy-done.9, bf16[256,160]{1,0:T(8,128)(2,1)S(1)} %bitcast.22, bf16[128,256]{1,0:T(8,128)(2,1)S(1)} %copy-done.5, ...), custom_call_target="tpu_custom_call" | custom-call | tf_op jit(solution)/shard_map/local/pallas_call | solution.py:286
  68.6 21.0 %all_to_all.33.got_ref = bf16[32,16,128]{2,1,0:T(8,128)(2,1)S(1)} all-to-all(bf16[32,16,128]{2,1,0:T(8,128)(2,1)S(1)} %get-tuple-element.23), channel_id=1, replica_groups=mesh['seq'=32,'chan'=16] {'seq'}, dimensions={0} | all-to-all | bytes 262144 | tf_op jit(solution)/shard_map/all_to_all | solution.py:328
  89.6 1.7 %chain.1 = (bf16[32,16,128]{2,1,0:T(8,128)(2,1)S(1)}, f32[4,8,16]{2,1,0:T(8,128)S(1)}) custom-call(s32[4]{0:T(128)S(1)} %copy-done.8, s32[4]{0:T(128)S(1)} %copy-done.9, bf16[32,16,128]{2,1,0:T(8,128)(2,1)S(1)} %all_to_all.33.got_ref, bf16[256,128]{1,0:T(8,128)(2,1)S(1)} %get-tuple-element.24.edge_ref, f32[16,256]{1,0:T(8,128)S(1)} %copy-done.6), custom_call_target="tpu_custom_call" | custom-call | tf_op jit(solution)/shard_map/chain/pallas_call | solution.py:286
  91.2 12.8 %all_to_all.34.back_ref = bf16[32,16,128]{2,1,0:T(8,128)(2,1)S(1)} all-to-all(bf16[32,16,128]{2,1,0:T(8,128)(2,1)S(1)} %get-tuple-element.25), channel_id=1, replica_groups=mesh['seq'=32,'chan'=16] {'seq'}, dimensions={0} | all-to-all | bytes 262144 | tf_op jit(solution)/shard_map/all_to_all | solution.py:328
  104.0 0.0 copy-done.1
  104.0 0.0 copy-done.13
  104.0 3.6 %output.1 = (bf16[128,256]{1,0:T(8,128)(2,1)S(1)}, bf16[128,2048]{1,0:T(8,128)(2,1)S(1)}, f32[8,128]{1,0:T(8,128)S(1)}) custom-call(bf16[32,16,128]{2,1,0:T(8,128)(2,1)S(1)} %all_to_all.34.back_ref, f32[2,256,128]{2,1,0:T(8,128)S(1)} %get-tuple-element.26.delta_ref, f32[2,256,128]{2,1,0:T(8,128)S(1)} %get-tuple-element.27.drive_ref, ...), custom_call_target="tpu_custom_call" | custom-call | tf_op jit(solution)/shard_map/output/pallas_call | solution.py:286
  107.6 4.6 %collective-permute-start.2 = (bf16[128,2048]{1,0:T(8,128)(2,1)S(1)}, bf16[128,2048]{1,0:T(8,128)(2,1)S(1)}, u32[]{:S(2)}, u32[]{:S(2)}) collective-permute-start(bf16[128,2048]{1,0:T(8,128)(2,1)S(1)} %get-tuple-element.32), channel_id=1, source_target_pairs={{0,1},{1,0},{2,3},{3,2},{4,5},{5,4},{6,7},{7,6},{8,9},{9,8},{10,11... | collective-permute-start | bytes 1572872 | tf_op jit(solution)/shard_map/ppermute | solution.py:410
  112.2 0.3 fusion
  112.5 0.0 copy-start.3
  112.5 1.2 collective-permute-done.2
  113.7 0.9 add_convert_fusion
  114.6 3.5 %all-to-all-start.5 = ((bf16[8,16,2048]{2,1,0:T(8,128)(2,1)}), bf16[8,16,2048]{2,1,0:T(8,128)(2,1)S(1)}, u32[]{:S(2)}, u32[]{:S(2)}) async-start(bf16[8,16,2048]{2,1,0:T(8,128)(2,1)} %bitcast.10), calls=%async_computation.5 | async-start | bytes 1048576 | tf_op jit(solution)/shard_map/all_to_all | solution.py:328
  118.1 0.6 copy.17
  118.7 0.7 copy.16
  119.4 16.6 %all-to-all-done.5.parts_ref = bf16[8,16,2048]{2,1,0:T(8,128)(2,1)S(1)} async-done(((bf16[8,16,2048]{2,1,0:T(8,128)(2,1)}), bf16[8,16,2048]{2,1,0:T(8,128)(2,1)S(1)}, u32[]{:S(2)}, u32[]{:S(2)}) %all-to-all-start.5) | async-done | bytes 524320 | tf_op jit(solution)/shard_map/all_to_all | solution.py:328
  136.0 0.0 copy-done.3
  136.0 0.7 final.1
  (3 shorter events, 0.0 us)
Async XLA Ops:
  0.6 0.8 copy-start.2
  1.5 0.7 copy-start.7
  2.3 33.3 %copy-start = (bf16[2,2048,256]{2,1,0:T(8,128)(2,1)S(1)}, bf16[2,2048,256]{2,1,0:T(8,128)(2,1)}, u32[]{:S(2)}) copy-start(bf16[2,2048,256]{2,1,0:T(8,128)(2,1)} %weight_ref.1) | copy-start | bytes 6291460
  2.3 33.3 %copy-start.8 = (s32[4]{0:T(128)S(1)}, s32[4]{0:T(128)}, u32[]{:S(2)}) copy-start(s32[4]{0:T(128)} %lengths_ref.7) | copy-start | bytes 52
  2.3 33.3 %copy-start.9 = (s32[4]{0:T(128)S(1)}, s32[4]{0:T(128)}, u32[]{:S(2)}) copy-start(s32[4]{0:T(128)} %order_ref.7) | copy-start | bytes 52
  29.2 6.4 %collective-permute-start = (bf16[128,2048]{1,0:T(8,128)(2,1)S(1)}, bf16[128,2048]{1,0:T(8,128)(2,1)S(1)}, u32[]{:S(2)}, u32[]{:S(2)}) collective-permute-start(bf16[128,2048]{1,0:T(8,128)(2,1)S(1)} %bitcast.29), channel_id=1, source_target_pairs={{0,1},{1,0},{2,3},{3,2},{4,5},{5,4},{6,7},{7,6},{8,9},{9,8},{10,11... | collective-permute-start | bytes 1572872 | tf_op jit(solution)/shard_map/ppermute | solution.py:332
  35.5 5.1 %copy-start.4 = (bf16[256,160]{0,1:T(8,128)(2,1)S(1)}, bf16[256,160]{0,1:T(8,128)(2,1)}, u32[]{:S(2)}) copy-start(bf16[256,160]{0,1:T(8,128)(2,1)} %param.18) | copy-start | bytes 245764
  35.5 5.1 %copy-start.10 = (f32[4,256]{1,0:T(4,128)S(1)}, f32[4,256]{1,0:T(4,128)}, u32[]{:S(2)}) copy-start(f32[4,256]{1,0:T(4,128)} %taps_ref.1) | copy-start | bytes 12292
  35.5 5.1 %copy-start.11 = (f32[256]{0:T(256)S(1)}, f32[256]{0:T(256)}, u32[]{:S(2)}) copy-start(f32[256]{0:T(256)} %param.17) | copy-start | bytes 3076
  35.6 29.9 %copy-start.5 = (bf16[128,256]{1,0:T(8,128)(2,1)S(1)}, bf16[128,256]{1,0:T(8,128)(2,1)}, u32[]{:S(2)}) copy-start(bf16[128,256]{1,0:T(8,128)(2,1)} %tm_ref.1) | copy-start | bytes 196612
  35.6 29.9 %copy-start.6 = (f32[16,256]{1,0:T(8,128)S(1)}, f32[16,256]{1,0:T(8,128)}, u32[]{:S(2)}) copy-start(f32[16,256]{1,0:T(8,128)} %alog_ref.3) | copy-start | bytes 49156
  35.6 29.9 %copy-start.12 = (f32[256]{0:T(256)S(1)}, f32[256]{0:T(256)}, u32[]{:S(2)}) copy-start(f32[256]{0:T(256)} %param.20) | copy-start | bytes 3076
  35.6 68.4 %copy-start.1 = (bf16[256,2048]{1,0:T(8,128)(2,1)S(1)}, bf16[256,2048]{1,0:T(8,128)(2,1)}, u32[]{:S(2)}) copy-start(bf16[256,2048]{1,0:T(8,128)(2,1)} %wout_ref.1) | copy-start | bytes 3145732
  35.6 68.4 %copy-start.13 = (f32[256]{0:T(256)S(1)}, f32[256]{0:T(256)}, u32[]{:S(2)}) copy-start(f32[256]{0:T(256)} %param.22) | copy-start | bytes 3076
  36.8 3.8 %collective-permute-start.1 = (bf16[8,256]{1,0:T(8,128)(2,1)S(1)}, bf16[8,256]{1,0:T(8,128)(2,1)S(1)}, u32[]{:S(2)}, u32[]{:S(2)}) collective-permute-start(bf16[8,256]{1,0:T(8,128)(2,1)S(1)} %get-tuple-element.20), channel_id=1, source_target_pairs={{0,16},{16,32},{32,48},{48,64},{64,80},{80,96},{96,112},{112,128},... | collective-permute-start | bytes 12296 | tf_op jit(solution)/shard_map/ppermute | solution.py:345
  107.6 6.1 %collective-permute-start.2 = (bf16[128,2048]{1,0:T(8,128)(2,1)S(1)}, bf16[128,2048]{1,0:T(8,128)(2,1)S(1)}, u32[]{:S(2)}, u32[]{:S(2)}) collective-permute-start(bf16[128,2048]{1,0:T(8,128)(2,1)S(1)} %get-tuple-element.32), channel_id=1, source_target_pairs={{0,1},{1,0},{2,3},{3,2},{4,5},{5,4},{6,7},{7,6},{8,9},{9,8},{10,11... | collective-permute-start | bytes 1572872 | tf_op jit(solution)/shard_map/ppermute | solution.py:410
  112.5 23.5 %copy-start.3 = (bf16[16,2048]{1,0:T(8,128)(2,1)S(1)}, bf16[16,2048]{1,0:T(8,128)(2,1)}, u32[]{:S(2)}) copy-start(bf16[16,2048]{1,0:T(8,128)(2,1)} %tokens_ref.3) | copy-start | bytes 196612
  114.6 21.4 %all-to-all-start.5 = ((bf16[8,16,2048]{2,1,0:T(8,128)(2,1)}), bf16[8,16,2048]{2,1,0:T(8,128)(2,1)S(1)}, u32[]{:S(2)}, u32[]{:S(2)}) async-start(bf16[8,16,2048]{2,1,0:T(8,128)(2,1)} %bitcast.10), calls=%async_computation.5 | async-start | bytes 1048576 | tf_op jit(solution)/shard_map/all_to_all | solution.py:328
